TPU v7x, 256 devices: a whole 4x4x8 slice. The times are simulated.
256 devices in a mesh: grp: 8 (over y, x_hi), tp: 32 (over z, x_lo, core).
Axes of the slice: x: 4 (x_hi: 2, x_lo: 2; x = x_hi * 2 + x_lo), y: 4, z: 8, core: 2. Of those that a mesh axis runs over, the one named last changes fastest.
Arguments:
- key_cache: bfloat16 [8, 32, 768, 512], P('grp', 'tp'), may hold values from -6 to 6
- value_cache: bfloat16 [8, 32, 768, 512], P('grp', 'tp'), may hold values from -12 to 12
- lengths: int32 [8, 32], P('grp', 'tp'), may hold values from 256 to 768, as said below
- queries: bfloat16 [8, 1, 32, 8192], P('grp', None, 'tp'), may hold values from -12 to 12
- new_keys: bfloat16 [8, 1, 32, 512], P('grp', None, 'tp'), may hold values from -18 to 18
- new_values: bfloat16 [8, 1, 32, 512], P('grp', None, 'tp'), may hold values from -12 to 12
- residual: bfloat16 [8, 1, 32, 8192], P('grp', None, 'tp'), may hold values from -4 to 4
- norm_gain: float32 [8192], replicated, may hold values from 0.25 to 1.75
- gate_weight: bfloat16 [8, 6656, 8192], P('grp', 'tp'), may hold values from -0.0625 to 0.0625
- up_weight: bfloat16 [8, 6656, 8192], P('grp', 'tp'), may hold values from -0.0625 to 0.0625
- down_weight: bfloat16 [8, 6656, 8192], P('grp', 'tp'), may hold values from -0.0390625 to 0.0390625
Outputs:
- mixed: bfloat16 [8, 1, 32, 8192], P('grp', None, 'tp')
Inputs may be any that keep to these rules, and one draw needn't show every extreme that they name: `lengths`: some row has exactly 768 valid positions.
All inputs are finite; a program needn't handle non-finite values.
Results may differ from a plain program's by a relative error of at most 0.005.
Values may be sent and summed in bfloat16 or wider, within the bound.
No kernel may reach another device: no remote copies, remote signals or barrier semaphores. Data moves between devices by JAX's collectives and lax.ppermute only.
A program may use at most 64 MiB of HBM per device.

v0:
```python
import jax
import jax.numpy as jnp
from jax import lax
from jax.sharding import Mesh
from jax.sharding import PartitionSpec as P

HEADS = 64
HD = 128
KVH = 4
TP = ("tp_0", "tp_1", "tp_2")
masked_score = -1e30


def in_order(pieces, dim):
    pieces = jnp.moveaxis(pieces, 0, dim)
    dims = pieces.shape
    return pieces.reshape(*dims[:dim], dims[dim] * dims[dim + 1], *dims[dim + 2 :])


def sent_to_all(value, axis):
    copies = jnp.broadcast_to(value, (lax.axis_size(axis), *value.shape))
    return lax.all_to_all(copies, axis, split_axis=0, concat_axis=0, tiled=True)


def collect(value, axis, dim):
    return in_order(sent_to_all(value, axis), dim)


def split_up(value, dim, size):
    before, after = (value.shape[:dim], value.shape[dim + 1 :])
    return jnp.moveaxis(value.reshape(*before, size, -1, *after), dim, 0)


def sum_at_owner(value, axis, dim):
    pieces = split_up(value, dim, lax.axis_size(axis))
    arrived = lax.all_to_all(pieces, axis, split_axis=0, concat_axis=0, tiled=True)
    return arrived.sum(axis=0)


def summed_rows(value, axes, dim):
    far, near = axes
    own = sum_at_owner(split_up(value, dim, lax.axis_size(far)), near, dim + 1)
    return jnp.sum(lax.all_to_all(own, far, 0, 0, tiled=True), axis=0)


def feed_rows(normed_rows, gate_weight, up_weight, down_weight):
    numbers = (((1,), (1,)), ((), ()))
    gate_part = lax.dot_general(
        normed_rows, gate_weight[0], numbers, preferred_element_type=jnp.float32
    )
    up_part = lax.dot_general(
        normed_rows, up_weight[0], numbers, preferred_element_type=jnp.float32
    )
    product = (jax.nn.silu(gate_part) * up_part).astype(jnp.bfloat16)
    return jnp.dot(product, down_weight[0], preferred_element_type=jnp.float32)


def local(
    key_cache,
    value_cache,
    lengths,
    queries,
    new_keys,
    new_values,
    residual,
    norm_gain,
    gate_weight,
    up_weight,
    down_weight,
):
    groups = lax.axis_size("grp")
    members = lax.axis_size(TP)
    serving = lax.axis_index("grp") < groups // 2
    step_count = queries.shape[1]
    own_rows = queries.shape[2]
    model_width = queries.shape[3]
    head_share = HEADS // KVH
    slot_count = key_cache.shape[2]
    score_scale = HD ** (-0.5)
    own_heads = queries[0].reshape(step_count, own_rows, KVH, head_share, HD)
    cache_keys = key_cache[0].reshape(own_rows, slot_count, KVH, HD)
    cache_values = value_cache[0].reshape(own_rows, slot_count, KVH, HD)
    positions = jnp.arange(slot_count)
    usable = positions[None, :] < lengths[0][:, None]
    usable_mask = usable[None, :, None, None, :]
    cache_scores = (
        jnp.einsum("srjgd,rpjd->srjgp", own_heads, cache_keys, preferred_element_type=jnp.float32)
        * score_scale
    )
    cache_scores = jnp.where(usable_mask, cache_scores, masked_score)
    fresh_keys = new_keys[0].reshape(step_count, own_rows, KVH, HD)
    fresh_values = new_values[0].reshape(step_count, own_rows, KVH, HD)
    fresh_scores = (
        jnp.einsum("srjgd,trjd->srjgt", own_heads, fresh_keys, preferred_element_type=jnp.float32)
        * score_scale
    )
    causal = jnp.arange(step_count)[:, None] >= jnp.arange(step_count)[None, :]
    causal_mask = causal[:, None, None, None, :]
    fresh_scores = jnp.where(causal_mask, fresh_scores, masked_score)
    ceiling = jnp.maximum(jnp.max(cache_scores, axis=-1), jnp.max(fresh_scores, axis=-1))
    cache_exp = jnp.where(usable_mask, jnp.exp(cache_scores - ceiling[..., None]), 0.0)
    fresh_exp = jnp.where(causal_mask, jnp.exp(fresh_scores - ceiling[..., None]), 0.0)
    denominator = jnp.sum(cache_exp, axis=-1) + jnp.sum(fresh_exp, axis=-1)
    cache_weighted = jnp.einsum(
        "srjgp,rpjd->srjgd",
        cache_exp.astype(jnp.bfloat16),
        cache_values,
        preferred_element_type=jnp.float32,
    )
    fresh_weighted = jnp.einsum(
        "srjgt,trjd->srjgd",
        fresh_exp.astype(jnp.bfloat16),
        fresh_values,
        preferred_element_type=jnp.float32,
    )
    attended = (cache_weighted + fresh_weighted) / denominator[..., None]
    attended = attended.reshape(step_count, own_rows, model_width)
    hidden = residual[0].astype(jnp.float32) + attended
    spread_sq = jnp.mean(hidden * hidden, axis=-1, keepdims=True)
    normed = (hidden * lax.rsqrt(spread_sq + 1e-05) * norm_gain).astype(jnp.bfloat16)
    block_rows = step_count * own_rows
    flat_rows = normed.reshape(block_rows, model_width)
    ffn_first = groups // 2
    group_block = collect(flat_rows, TP, 0).reshape(members, block_rows, model_width)
    all_rows = lax.all_gather(group_block, "grp", axis=1, tiled=True)
    real_rows = all_rows[:, : ffn_first * block_rows].reshape(
        members * ffn_first * block_rows, model_width
    )
    within = summed_rows(
        lax.cond(
            serving,
            lambda operand: jnp.zeros(
                (ffn_first * block_rows * lax.axis_size(TP), model_width), jnp.float32
            ),
            lambda operand: feed_rows(operand, gate_weight, up_weight, down_weight),
            real_rows,
        ),
        (("tp_0", "tp_1"), "tp_2"),
        0,
    )
    padded = jnp.concatenate(
        [within, jnp.zeros(((groups - ffn_first) * block_rows, model_width), jnp.float32)], 0
    )
    summed = sum_at_owner(padded, "grp", 0)
    mixed = (hidden + summed.reshape(step_count, own_rows, model_width)).astype(jnp.bfloat16)
    mixed = jnp.where(serving, mixed, jnp.zeros_like(mixed))
    return mixed[None]


def solution(mesh):
    finer = Mesh(mesh.devices.reshape(mesh.shape["grp"], 8, 2, 2), ("grp", "tp_0", "tp_1", "tp_2"))
    in_specs = (
        P("grp", TP, None, None),
        P("grp", TP, None, None),
        P("grp", TP),
        P("grp", None, TP, None),
        P("grp", None, TP, None),
        P("grp", None, TP, None),
        P("grp", None, TP, None),
        P(),
        P("grp", TP, None),
        P("grp", TP, None),
        P("grp", TP, None),
    )
    out_specs = P("grp", None, TP, None)
    return jax.shard_map(local, mesh=finer, in_specs=in_specs, out_specs=out_specs, check_vma=False)
```

profile of v0, /device:TPU:8, one launch (start us, length us, event | category | flops | bytes accessed | tf_op | source)
XLA Modules:
  0.0 242.3 jit_solution(11971909050703647324)
XLA Ops:
  7.3 0.7 convert.12
  8.0 0.8 convert_element_type.47
  8.8 1.8 reshape.147
  10.6 0.8 fusion.37
  11.4 0.4 fusion.41
  12.2 0.9 fusion.36
  13.9 0.9 broadcast_in_dim.51
  14.8 0.5 broadcast.47
  15.3 3.8 %reduce.6 = bf16[32,8192]{1,0:T(8,128)(2,1)S(1)} reduce(bf16[32,1,8192]{2,1,0:T(2,128)(2,1)S(1)} %broadcast_in_dim.51, bf16[]{:T(256)} %broadcast.47), dimensions={1}, to_apply=%broadcast_in_dim.51.reduce_sub_computation | reduce | bytes 1048578 | tf_op jit(solution)/shard_map/broadcast_in_dim | solution.py:21
  19.1 0.4 reshape.166
  19.5 27.6 %all_to_all.20 = bf16[32,2,4096]{2,1,0:T(2,128)(2,1)S(1)} all-to-all(bf16[32,2,4096]{2,1,0:T(2,128)(2,1)S(1)} %reshape.166), channel_id=1, replica_groups=mesh['grp'=8,'tp_0'=8,'tp_1'=2,'tp_2'=2] {'tp_0','tp_1','tp_2'}, dimensions={0} | all-to-all | bytes 1048576 | tf_op jit(solution)/shard_map/all_to_all | solution.py:22
  47.1 0.5 reshape.167
  47.7 1.4 copy.37
  49.1 71.8 %all-gather.2.cloned.1.call-done = bf16[32,8,8192]{2,0,1:T(8,128)(2,1)} async-done(((bf16[32,1,8192]{2,0,1:T(8,128)(2,1)}), bf16[32,8,8192]{2,0,1:T(8,128)(2,1)}) %all-gather.2.cloned.1.call-update) | async-done | bytes 4194320 | tf_op jit(solution)/shard_map/all_gather | solution.py:125
  120.8 2.4 conditional.1
  120.8 2.4 broadcast.43
  123.2 5.2 %reshape_reshape.3 = f32[16,2,4,8192]{3,2,1,0:T(4,128)} reshape(f32[128,8192]{1,0:T(8,128)} %get-tuple-element.54) | data formatting | bytes 8388608 | tf_op jit(solution)/shard_map/reshape;reshape | solution.py:31
  128.4 2.5 %copy.39 = f32[2,16,4,8192]{3,2,1,0:T(4,128)S(1)} copy(f32[2,16,4,8192]{3,2,0,1:T(4,128)} %bitcast.67) | data formatting | bytes 8388608 | tf_op jit(solution)/shard_map/transpose | solution.py:31
  130.9 8.2 %all_to_all.21 = f32[2,16,4,8192]{3,2,1,0:T(4,128)} all-to-all(f32[2,16,4,8192]{3,2,1,0:T(4,128)S(1)} %copy.39), channel_id=1, replica_groups=mesh['grp'=8,'tp_0'=8,'tp_1'=2,'tp_2'=2] {'tp_2'}, dimensions={0} | all-to-all | bytes 8388608 | tf_op jit(solution)/shard_map/all_to_all | solution.py:36
  139.1 4.0 %reduce_sum.51 = f32[16,4,8192]{2,1,0:T(4,128)S(1)} reduce(f32[2,16,4,8192]{3,2,1,0:T(4,128)} %all_to_all.21, f32[]{:T(128)} %constant.30.clone.1), dimensions={0}, to_apply=%region_5.6 | reduce | flops 524288 | bytes 6291460 | tf_op jit(solution)/shard_map/reduce_sum | solution.py:37
  143.1 58.7 %all_to_all.22 = f32[16,4,8192]{2,1,0:T(4,128)} all-to-all(f32[16,4,8192]{2,1,0:T(4,128)S(1)} %reduce_sum.51), channel_id=1, replica_groups=mesh['grp'=8,'tp_0'=8,'tp_1'=2,'tp_2'=2] {'tp_0','tp_1'}, dimensions={0} | all-to-all | bytes 4194304 | tf_op jit(solution)/shard_map/all_to_all | solution.py:43
  201.7 1.9 reduce_sum.52
  204.0 30.6 %all_to_all.23 = f32[8,1,8192]{2,1,0:T(1,128)S(1)} all-to-all(f32[8,1,8192]{2,1,0:T(1,128)S(1)} %copy.41), channel_id=1, replica_groups=mesh['grp'=8,'tp_0'=8,'tp_1'=2,'tp_2'=2] {'grp'}, dimensions={0} | all-to-all | bytes 524288 | tf_op jit(solution)/shard_map/all_to_all | solution.py:36
  234.8 0.7 broadcast_select_fusion
  (20 shorter events, 1.0 us)
Async XLA Ops:
  6.5 4.0 %copy-start = (bf16[1,1,1,8192]{3,2,1,0:T(2,128)(2,1)S(1)}, bf16[1,1,1,8192]{3,2,1,0:T(2,128)(2,1)}, u32[]{:S(2)}) copy-start(bf16[1,1,1,8192]{3,2,1,0:T(2,128)(2,1)} %param.16) | copy-start | bytes 49156
  6.5 5.5 %copy-start.1 = (bf16[1,1,768,512]{3,2,1,0:T(8,128)(2,1)S(1)}, bf16[1,1,768,512]{3,2,1,0:T(8,128)(2,1)}, u32[]{:S(2)}) copy-start(bf16[1,1,768,512]{3,2,1,0:T(8,128)(2,1)} %param.14) | copy-start | bytes 2359300
  6.5 7.3 %copy-start.3 = (f32[8192]{0:T(1024)S(1)}, f32[8192]{0:T(1024)}, u32[]{:S(2)}) copy-start(f32[8192]{0:T(1024)} %param.20) | copy-start | bytes 98308
  6.5 114.3 %all-gather.2.cloned.1.call-start = ((), (), s32[]{:S(2)}) async-start(), calls=%async_computation.4 | async-start | bytes 4718592 | tf_op jit(solution)/shard_map/all_gather | solution.py:125
  143.1 91.7 %copy-start.2 = (bf16[1,1,1,8192]{3,2,1,0:T(2,128)(2,1)S(1)}, bf16[1,1,1,8192]{3,2,1,0:T(2,128)(2,1)}, u32[]{:S(2)}) copy-start(bf16[1,1,1,8192]{3,2,1,0:T(2,128)(2,1)} %param.19) | copy-start | bytes 49156
Sparse Core Ops, SparseCore 0:
  49.2 71.6 all-gather.1
where the time goes:
time: 243 us; the launch traced here: 242 us
  blocking collectives  125 us (51%)
  waiting for transfers between devices  71.8 us (30%)
  local copies, waits for them, and re-layouts  16 us (7%)
  between operations  15 us (6%)
  other arithmetic  12.4 us (5%)
    all_gather x1, waiting for transfers between devices, local(): all_rows = lax.all_gather(group_block, 'grp', axis=1, tiled=True)  71.8 us
    all_to_all x1, blocking collectives, summed_rows(): return jnp.sum(lax.all_to_all(own, far, 0, 0, tiled=True), axis=0)  58.7 us
    all_to_all x2, blocking collectives, sum_at_owner(): lax.all_to_all(pieces, axis, split_axis=0, concat_axis=0, tiled=True)  38.8 us
    all_to_all x1, blocking collectives, sent_to_all(): return lax.all_to_all(copies, axis, split_axis=0, concat_axis=0, tiled=True)  27.6 us
    another operation x1, local copies, waits for them, and re-layouts, split_up(): return jnp.moveaxis(value.reshape(*before, size, -1, *after), dim, 0)  5.17 us
  transfers between devices with their start and end apart: 1, of which 1 were waited for; matrix products, arithmetic and copies ran while one was open for 0% of the time, Pallas kernels for 0%

commit v1 on v0

--- a/solution.py
+++ b/solution.py
@@ -122,7 +122,9 @@
     flat_rows = normed.reshape(block_rows, model_width)
     ffn_first = groups // 2
     group_block = collect(flat_rows, TP, 0).reshape(members, block_rows, model_width)
-    all_rows = lax.all_gather(group_block, "grp", axis=1, tiled=True)
+    all_rows = jnp.concatenate(
+        lax.all_to_all(jnp.stack([group_block] * lax.axis_size("grp")), "grp", 0, 0), axis=1
+    )
     real_rows = all_rows[:, : ffn_first * block_rows].reshape(
         members * ffn_first * block_rows, model_width
     )

time: 243 us -> 211 us (0.87)
  waiting for transfers between devices: 71.8 us -> 48.4 us
  between operations: 15 us -> 1.58 us
  starting transfers between devices: 0.01 us -> 7.08 us
  blocking collectives: 125 us -> 120 us
    all_gather x1 -> x0, waiting for transfers between devices: 71.8 us -> none  [local(): all_rows = lax.all_gather(group_block, 'grp', axis=1, tiled=True)]
    all_to_all x0 -> x1, waiting for transfers between devices: none -> 48.4 us  [local(): lax.all_to_all(jnp.stack([group_block] * lax.axis_size('grp')), 'grp', 0, 0)]
    all_to_all x0 -> x1, starting transfers between devices: none -> 7.08 us  [local(): lax.all_to_all(jnp.stack([group_block] * lax.axis_size('grp')), 'grp', 0, 0)]
    all_to_all x1, blocking collectives: 58.7 us -> 55.2 us  [summed_rows(): return jnp.sum(lax.all_to_all(own, far, 0, 0, tiled=True), axis=0)]
    another operation x3 -> x4, local copies, waits for them, and re-layouts: 4.34 us -> 6.8 us
where the time goes in v1:
time: 211 us; the launch traced here: 209 us
  blocking collectives  120 us (57%)
  waiting for transfers between devices  48.4 us (23%)
  local copies, waits for them, and re-layouts  17.7 us (8%)
  other arithmetic  12.4 us (6%)
  starting transfers between devices  7.08 us (3%)
    all_to_all x1, blocking collectives, summed_rows(): return jnp.sum(lax.all_to_all(own, far, 0, 0, tiled=True), axis=0)  55.2 us
    all_to_all x1, waiting for transfers between devices, local(): lax.all_to_all(jnp.stack([group_block] * lax.axis_size('grp')), 'grp', 0, 0)  48.4 us
    all_to_all x2, blocking collectives, sum_at_owner(): lax.all_to_all(pieces, axis, split_axis=0, concat_axis=0, tiled=True)  37.3 us
    all_to_all x1, blocking collectives, sent_to_all(): return lax.all_to_all(copies, axis, split_axis=0, concat_axis=0, tiled=True)  27.6 us
    all_to_all x1, starting transfers between devices, local(): lax.all_to_all(jnp.stack([group_block] * lax.axis_size('grp')), 'grp', 0, 0)  7.08 us
    another operation x1, local copies, waits for them, and re-layouts, split_up(): return jnp.moveaxis(value.reshape(*before, size, -1, *after), dim, 0)  5.17 us
    another operation x3, local copies, waits for them, and re-layouts  4.34 us
  transfers between devices with their start and end apart: 1, of which 1 were waited for; matrix products, arithmetic and copies ran while one was open for 0% of the time, Pallas kernels for 0%

profile of v1, /device:TPU:8, one launch (start us, length us, event | category | flops | bytes accessed | tf_op | source)
XLA Modules:
  0.0 209.4 jit_solution(17272455517633793147)
XLA Ops:
  0.7 0.7 convert.12
  1.4 0.8 convert_element_type.47
  2.2 1.8 reshape.156
  4.1 0.8 fusion.37
  5.7 0.9 fusion.36
  7.3 0.9 broadcast_in_dim.51
  8.3 0.5 broadcast.50
  8.8 3.8 %reduce.6 = bf16[32,8192]{1,0:T(8,128)(2,1)S(1)} reduce(bf16[32,1,8192]{2,1,0:T(2,128)(2,1)S(1)} %broadcast_in_dim.51, bf16[]{:T(256)} %broadcast.50), dimensions={1}, to_apply=%broadcast_in_dim.51.reduce_sub_computation | reduce | bytes 1048578 | tf_op jit(solution)/shard_map/broadcast_in_dim | solution.py:21
  13.0 27.6 %all_to_all.28 = bf16[32,2,4096]{2,1,0:T(2,128)(2,1)S(1)} all-to-all(bf16[32,2,4096]{2,1,0:T(2,128)(2,1)S(1)} %reshape.178), channel_id=1, replica_groups=mesh['grp'=8,'tp_0'=8,'tp_1'=2,'tp_2'=2] {'tp_0','tp_1','tp_2'}, dimensions={0} | all-to-all | bytes 1048576 | tf_op jit(solution)/shard_map/all_to_all | solution.py:22
  40.6 0.5 reshape.179
  41.1 0.6 copy.52
  41.7 2.5 %stack.3 = bf16[8,32,1,8192]{3,1,2,0:T(8,128)(2,1)} broadcast(bf16[32,8192]{1,0:T(8,128)(2,1)S(1)} %bitcast.76), dimensions={1,3} | broadcast | bytes 4718592 | tf_op jit(solution)/shard_map/stack | solution.py:126
  44.2 7.1 %all-to-all-start.1 = ((bf16[8,32,1,8192]{3,1,2,0:T(8,128)(2,1)}), bf16[8,32,1,8192]{3,1,2,0:T(8,128)(2,1)}, u32[]{:S(2)}, u32[]{:S(2)}) async-start(bf16[8,32,1,8192]{3,1,2,0:T(8,128)(2,1)} %stack.3), calls=%async_computation.1 | async-start | bytes 8388608 | tf_op jit(solution)/shard_map/all_to_all | solution.py:126
  51.3 48.4 %all-to-all-done.1 = bf16[8,32,1,8192]{3,1,2,0:T(8,128)(2,1)} async-done(((bf16[8,32,1,8192]{3,1,2,0:T(8,128)(2,1)}), bf16[8,32,1,8192]{3,1,2,0:T(8,128)(2,1)}, u32[]{:S(2)}, u32[]{:S(2)}) %all-to-all-start.1) | async-done | bytes 4194336 | tf_op jit(solution)/shard_map/all_to_all | solution.py:126
  99.7 2.4 %conditional.1 = (f32[128,8192]{1,0:T(8,128)}) conditional(s32[]{:T(128)} %convert_element_type.50, (bf16[1,208,8192]{2,1,0:T(8,128)(2,1)}, bf16[32,8,1,8192]{3,0,2,1:T(8,128)(2,1)}, bf16[1,208,8192]{2,1,0:T(8,128)(2,1)}, bf16[1,208,8192]{2,1,0:T(8,128)(2,1)}) %tuple.11, () %tuple.12), branch_computations={%region_3.4_spmd, %region_4.5_spmd} | conditional | flops 1308782592 | bytes 35602440 | solution.py:132
  99.7 2.4 %broadcast.46 = f32[128,8192]{1,0:T(8,128)} broadcast(f32[]{:T(128)} %constant.12.clone), dimensions={} | broadcast | bytes 4194308 | tf_op jit(solution)/shard_map/broadcast.3
  102.1 5.2 %reshape_reshape.3 = f32[16,2,4,8192]{3,2,1,0:T(4,128)} reshape(f32[128,8192]{1,0:T(8,128)} %get-tuple-element.51) | data formatting | bytes 8388608 | tf_op jit(solution)/shard_map/reshape;reshape | solution.py:31
  107.2 2.5 %copy.34 = f32[2,16,4,8192]{3,2,1,0:T(4,128)S(1)} copy(f32[2,16,4,8192]{3,2,0,1:T(4,128)} %bitcast.74) | data formatting | bytes 8388608 | tf_op jit(solution)/shard_map/transpose | solution.py:31
  109.7 8.2 %all_to_all.29 = f32[2,16,4,8192]{3,2,1,0:T(4,128)} all-to-all(f32[2,16,4,8192]{3,2,1,0:T(4,128)S(1)} %copy.34), channel_id=1, replica_groups=mesh['grp'=8,'tp_0'=8,'tp_1'=2,'tp_2'=2] {'tp_2'}, dimensions={0} | all-to-all | bytes 8388608 | tf_op jit(solution)/shard_map/all_to_all | solution.py:36
  117.9 4.0 %reduce_sum.51 = f32[16,4,8192]{2,1,0:T(4,128)S(1)} reduce(f32[2,16,4,8192]{3,2,1,0:T(4,128)} %all_to_all.29, f32[]{:T(128)} %constant.30.clone.1), dimensions={0}, to_apply=%region_5.6 | reduce | flops 524288 | bytes 6291460 | tf_op jit(solution)/shard_map/reduce_sum | solution.py:37
  121.9 55.2 %all_to_all.30 = f32[16,4,8192]{2,1,0:T(4,128)} all-to-all(f32[16,4,8192]{2,1,0:T(4,128)S(1)} %reduce_sum.51), channel_id=1, replica_groups=mesh['grp'=8,'tp_0'=8,'tp_1'=2,'tp_2'=2] {'tp_0','tp_1'}, dimensions={0} | all-to-all | bytes 4194304 | tf_op jit(solution)/shard_map/all_to_all | solution.py:43
  177.1 1.9 reduce_sum.52
  179.4 29.1 %all_to_all.31 = f32[8,1,8192]{2,1,0:T(1,128)S(1)} all-to-all(f32[8,1,8192]{2,1,0:T(1,128)S(1)} %copy.36), channel_id=1, replica_groups=mesh['grp'=8,'tp_0'=8,'tp_1'=2,'tp_2'=2] {'grp'}, dimensions={0} | all-to-all | bytes 524288 | tf_op jit(solution)/shard_map/all_to_all | solution.py:36
  208.7 0.7 broadcast_select_fusion
  (20 shorter events, 1.8 us)
Async XLA Ops:
  0.0 4.0 %copy-start = (bf16[1,1,1,8192]{3,2,1,0:T(2,128)(2,1)S(1)}, bf16[1,1,1,8192]{3,2,1,0:T(2,128)(2,1)}, u32[]{:S(2)}) copy-start(bf16[1,1,1,8192]{3,2,1,0:T(2,128)(2,1)} %param.16) | copy-start | bytes 49156
  0.0 5.5 %copy-start.1 = (bf16[1,1,768,512]{3,2,1,0:T(8,128)(2,1)S(1)}, bf16[1,1,768,512]{3,2,1,0:T(8,128)(2,1)}, u32[]{:S(2)}) copy-start(bf16[1,1,768,512]{3,2,1,0:T(8,128)(2,1)} %param.14) | copy-start | bytes 2359300
  0.0 7.3 %copy-start.3 = (f32[8192]{0:T(1024)S(1)}, f32[8192]{0:T(1024)}, u32[]{:S(2)}) copy-start(f32[8192]{0:T(1024)} %param.20) | copy-start | bytes 98308
  44.2 55.5 %all-to-all-start.1 = ((bf16[8,32,1,8192]{3,1,2,0:T(8,128)(2,1)}), bf16[8,32,1,8192]{3,1,2,0:T(8,128)(2,1)}, u32[]{:S(2)}, u32[]{:S(2)}) async-start(bf16[8,32,1,8192]{3,1,2,0:T(8,128)(2,1)} %stack.3), calls=%async_computation.1 | async-start | bytes 8388608 | tf_op jit(solution)/shard_map/all_to_all | solution.py:126
  121.9 86.8 %copy-start.2 = (bf16[1,1,1,8192]{3,2,1,0:T(2,128)(2,1)S(1)}, bf16[1,1,1,8192]{3,2,1,0:T(2,128)(2,1)}, u32[]{:S(2)}) copy-start(bf16[1,1,1,8192]{3,2,1,0:T(2,128)(2,1)} %param.19) | copy-start | bytes 49156
